TPU v7x, 512 devices: a whole 4x8x8 slice. The times are simulated.
512 devices in a mesh: samp: 8 (over z), pair: 16 (over y_lo, x), recv: 4 (over y_hi, core).
Axes of the slice: x: 4, y: 8 (y_hi: 2, y_lo: 4; y = y_hi * 4 + y_lo), z: 8, core: 2. Of those that a mesh axis runs over, the one named last changes fastest.
Arguments:
- cell_expression: bfloat16 [32, 16384, 2048], P('samp', 'recv', 'pair'), may hold values from 0 to 24
- cell_labels: int32 [32, 16384], P('samp', 'recv'), may hold values from 0 to 127, as said below
- ligand_gene: int32 [2048], P('pair'), may hold values from 0 to 2047
- receptor_gene: int32 [2048], P('pair'), may hold values from 0 to 2047
- pair_factor: bfloat16 [2048, 32], P('pair'), may hold values from -0.53033009 to 0.53033009
- sender_factor: bfloat16 [128, 32], replicated, may hold values from -0.5 to 0.5
- receiver_factor: bfloat16 [128, 32], P('recv'), may hold values from -2.5 to 2.5
Outputs:
- sample_factor: float32 [32, 32], P('samp')
Inputs may be any that keep to these rules, and one draw needn't show every extreme that they name: `cell_labels`: in every sample one cell type has no cell.
All inputs are finite; a program needn't handle non-finite values.
Results may differ from a plain program's by a relative error of at most 0.0051.
Values may be sent and summed in bfloat16 or wider, within the bound.
No kernel may reach another device: no remote copies, remote signals or barrier semaphores. Data moves between devices by JAX's collectives and lax.ppermute only.
A program may use at most 64 MiB of HBM per device.

v0:
```python
import jax
import jax.numpy as jnp
from jax import lax
from jax.sharding import PartitionSpec as P


def body(
    cell_expression,
    cell_labels,
    ligand_gene,
    receptor_gene,
    pair_factor,
    sender_factor,
    receiver_factor,
):
    clusters = sender_factor.shape[0]
    factor_rank = sender_factor.shape[1]
    block_width = receiver_factor.shape[0]
    member = (
        cell_labels[:, :, None] == jnp.arange(clusters, dtype=jnp.int32)[None, None, :]
    ).astype(jnp.bfloat16)
    part_sums = jnp.einsum(
        "scg,sck->sgk", cell_expression, member, preferred_element_type=jnp.float32
    )
    part_counts = jnp.sum(member, axis=1, dtype=jnp.float32)
    receiver_start = lax.axis_index("recv") * block_width
    cluster_total, cell_count = lax.psum((part_sums, part_counts), "recv")
    cluster_mean = (cluster_total / jnp.maximum(cell_count, 1.0)[:, None, :]).astype(jnp.bfloat16)
    segment = lax.all_gather(cluster_mean, "pair", axis=1, tiled=True)
    ligand_table = jnp.einsum(
        "sga,ar->srg", segment, sender_factor, preferred_element_type=jnp.float32
    ).astype(jnp.bfloat16)
    receiver_columns = lax.dynamic_slice_in_dim(segment, receiver_start, block_width, 2)
    receptor_table = jnp.einsum(
        "sgb,br->srg", receiver_columns, receiver_factor, preferred_element_type=jnp.float32
    ).astype(jnp.bfloat16)
    joined_tables = jnp.concatenate([ligand_table, receptor_table], axis=1)
    ligand_rows = jnp.take(joined_tables[:, :factor_rank, :], ligand_gene, axis=2).astype(
        jnp.float32
    )
    receptor_rows = jnp.take(joined_tables[:, factor_rank:, :], receptor_gene, axis=2).astype(
        jnp.float32
    )
    pair_weights = pair_factor.astype(jnp.float32).T
    partial_product = jnp.sum(ligand_rows * receptor_rows * pair_weights[None, :, :], axis=2)
    pair_gram = jnp.einsum(
        "pr,pq->rq", pair_factor, pair_factor, preferred_element_type=jnp.float32
    )
    sender_gram = jnp.einsum(
        "pr,pq->rq", sender_factor, sender_factor, preferred_element_type=jnp.float32
    )
    receiver_gram = jnp.einsum(
        "pr,pq->rq", receiver_factor, receiver_factor, preferred_element_type=jnp.float32
    )
    product_total = lax.psum(partial_product, ("pair", "recv"))
    pair_gram = lax.psum(pair_gram, "pair")
    receiver_gram = lax.psum(receiver_gram, "recv")
    hadamard = pair_gram * sender_gram * receiver_gram
    cholesky_factor = jnp.linalg.cholesky(hadamard)
    solution = jax.scipy.linalg.cho_solve((cholesky_factor, True), product_total.T)
    return solution.T


def solution(mesh):
    placed = (
        P("samp", "recv", "pair"),
        P("samp", "recv"),
        P("pair"),
        P("pair"),
        P("pair", None),
        P(),
        P("recv", None),
    )
    return jax.shard_map(
        body, mesh=mesh, in_specs=placed, out_specs=P("samp", None), check_vma=False
    )
```

profile of v0, /device:TPU:9, one launch (start us, length us, event | category | flops | bytes accessed | tf_op | source)
XLA Modules:
  0.0 325.3 jit_solution(4889094992332328623)
XLA Ops:
  6.6 0.0 all-reduce.3.cloned.1.call-start
  6.6 4.6 %fusion.3 = f32[4,128,128]{1,2,0:T(8,128)} fusion(bf16[4,4096,128]{2,1,0:T(8,128)(2,1)} %param.9, s32[4,4096]{1,0:T(4,128)} %param.10), kind=kOutput, calls=%fused_computation.9 | convolution fusion | flops 538968064 | bytes 4521984 | tf_op jit(solution)/shard_map/scg,sck->sgk/dot_general | solution.py:22
  11.2 0.0 all-reduce.3.cloned.1.call-update
  11.2 0.0 all-gather.2.cloned.1.call-start
  11.3 0.2 fusion.16
  11.5 1.3 convert_reduce_fusion
  12.8 18.3 %all-reduce = (f32[4,128]{1,0:T(4,128)S(1)}, f32[32,32]{0,1:T(8,128)S(1)}) all-reduce(f32[4,128]{1,0:T(4,128)S(1)} %convert_reduce_fusion, f32[32,32]{0,1:T(8,128)S(1)} %fusion.16), channel_id=1, replica_groups=mesh['samp'=8,'pair'=16,'recv'=4] {'recv'}, use_global_device_ids=true, to_apply=%region_6.7 | all-reduce | flops 1536 | bytes 12288 | tf_op jit(solution)/shard_map/psum | solution.py:27
  31.0 43.7 %all-reduce.3.cloned.1.call-done = f32[4,128,128]{1,2,0:T(8,128)} async-done(((f32[4,128,128]{1,2,0:T(8,128)}), f32[4,128,128]{1,2,0:T(8,128)}) %all-reduce.3.cloned.1.call-update) | async-done | bytes 262160 | tf_op jit(solution)/shard_map/psum | solution.py:27
  74.7 1.7 divide_convert_fusion
  76.4 0.0 all-gather.2.cloned.1.call-update
  76.5 0.0 copy-done.1
  76.5 0.1 fusion.15
  76.6 57.9 %psum.35 = f32[32,32]{0,1:T(8,128)S(1)} all-reduce(f32[32,32]{0,1:T(8,128)S(1)} %fusion.15), channel_id=1, replica_groups=mesh['samp'=8,'pair'=16,'recv'=4] {'pair'}, use_global_device_ids=true, to_apply=%region_0.0 | all-reduce | flops 1024 | bytes 8192 | tf_op jit(solution)/shard_map/psum | solution.py:56
  134.5 0.1 fusion.4
  134.6 0.1 copy.16
  134.7 2.9 cholesky.16
  137.6 0.6 compare_reduce_fusion
  138.3 0.7 fusion.6
  138.9 2.5 custom-call.10
  141.4 0.1 copy.17
  141.5 0.0 copy-done.5
  141.6 0.3 all-gather.2.cloned.1.call-done
  141.8 2.0 convolution_convert_fusion
  143.8 1.4 copy.23
  145.2 1.4 convolution_convert_fusion.1
  146.6 2.5 copy.24
  149.1 0.7 gather_fusion
  149.9 2.3 gather_fusion.1
  152.2 0.3 multiply_reduce_fusion
  152.6 164.9 %psum.39 = f32[4,32]{1,0:T(4,128)S(1)} all-reduce(f32[4,32]{1,0:T(4,128)S(1)} %multiply_reduce_fusion), channel_id=1, replica_groups=mesh['samp'=8,'pair'=16,'recv'=4] {'pair','recv'}, use_global_device_ids=true, to_apply=%region_8.10 | all-reduce | flops 128 | bytes 1024 | tf_op jit(solution)/shard_map/psum | solution.py:55
  317.5 0.2 fusion.9
  317.7 0.8 fusion.7
  (19 shorter events, 0.1 us)
Async XLA Ops:
  6.5 127.9 %copy-start = (bf16[128,32]{0,1:T(8,128)(2,1)S(1)}, bf16[128,32]{0,1:T(8,128)(2,1)}, u32[]{:S(2)}) copy-start(bf16[128,32]{0,1:T(8,128)(2,1)} %param.14) | copy-start | bytes 24580
  6.5 4.9 %copy-start.2 = (s32[4,4096]{1,0:T(4,128)S(1)}, s32[4,4096]{1,0:T(4,128)}, u32[]{:S(2)}) copy-start(s32[4,4096]{1,0:T(4,128)} %param.10) | copy-start | bytes 196612
  6.5 4.7 %copy-start.3 = (bf16[32,32]{1,0:T(8,128)(2,1)S(1)}, bf16[32,32]{1,0:T(8,128)(2,1)}, u32[]{:S(2)}) copy-start(bf16[32,32]{1,0:T(8,128)(2,1)} %param.15) | copy-start | bytes 6148
  6.5 69.9 %copy-start.1 = (bf16[128,32]{0,1:T(8,128)(2,1)S(1)}, bf16[128,32]{0,1:T(8,128)(2,1)}, u32[]{:S(2)}) copy-start(bf16[128,32]{0,1:T(8,128)(2,1)} %param.13) | copy-start | bytes 24580
  6.5 134.9 %copy-start.4 = (s32[128]{0:T(128)S(1)}, s32[128]{0:T(128)}, u32[]{:S(2)}) copy-start(s32[128]{0:T(128)} %param.12) | copy-start | bytes 1540
  6.5 135.0 %copy-start.5 = (s32[128]{0:T(128)S(1)}, s32[128]{0:T(128)}, u32[]{:S(2)}) copy-start(s32[128]{0:T(128)} %param.11) | copy-start | bytes 1540
  6.6 68.1 %all-reduce.3.cloned.1.call-start = ((), (), s32[]{:S(2)}) async-start(), calls=%async_computation | async-start | bytes 524288 | tf_op jit(solution)/shard_map/psum | solution.py:27
  11.2 130.6 %all-gather.2.cloned.1.call-start = ((), (), s32[]{:S(2)}) async-start(), calls=%async_computation.1 | async-start | bytes 2228224 | tf_op jit(solution)/shard_map/all_gather | solution.py:29
Sparse Core Ops, SparseCore 0:
  11.3 63.2 all-reduce.2
  76.9 64.9 all-gather.1
where the time goes:
time: 326 us; the launch traced here: 325 us
  blocking collectives  241 us (74%)
  waiting for transfers between devices  43.9 us (13%)
  between operations  13.6 us (4%)
  other arithmetic  10.1 us (3%)
  matrix products  9.4 us (3%)
  local copies, waits for them, and re-layouts  7.17 us (2%)
    psum x1, blocking collectives, body(): product_total = lax.psum(partial_product, ('pair', 'recv'))  165 us
    psum x1, blocking collectives, body(): pair_gram = lax.psum(pair_gram, 'pair')  57.9 us
    psum x1, waiting for transfers between devices, body(): cluster_total, cell_count = lax.psum((part_sums, part_counts), 'recv')  43.7 us
    psum x1, blocking collectives, body(): cluster_total, cell_count = lax.psum((part_sums, part_counts), 'recv')  18.3 us
  transfers between devices with their start and end apart: 2, of which 2 were waited for; matrix products, arithmetic and copies ran while one was open for 3% of the time, Pallas kernels for 0%

commit v1 on v0

--- a/solution.py
+++ b/solution.py
@@ -52,7 +52,7 @@
     receiver_gram = jnp.einsum(
         "pr,pq->rq", receiver_factor, receiver_factor, preferred_element_type=jnp.float32
     )
-    product_total = lax.psum(partial_product, ("pair", "recv"))
+    product_total = lax.psum(lax.psum(partial_product, "pair"), "recv")
     pair_gram = lax.psum(pair_gram, "pair")
     receiver_gram = lax.psum(receiver_gram, "recv")
     hadamard = pair_gram * sender_gram * receiver_gram

time: 326 us -> 274 us (0.84)
  the two profiles are of different devices: /device:TPU:9 before, /device:TPU:1 now
where the time goes in v1:
time: 274 us
  blocking collectives  122 us (45%)
  waiting for transfers between devices  112 us (41%)
  between operations  13.6 us (5%)
  other arithmetic  10.1 us (4%)
  matrix products  9.45 us (3%)
  local copies, waits for them, and re-layouts  7.16 us (3%)
    psum x2, blocking collectives, body(): product_total = lax.psum(lax.psum(partial_product, 'pair'), 'recv')  106 us
    all_gather x1, waiting for transfers between devices, body(): segment = lax.all_gather(cluster_mean, 'pair', axis=1, tiled=True)  63.7 us
    psum x1, waiting for transfers between devices, body(): cluster_total, cell_count = lax.psum((part_sums, part_counts), 'recv')  48.2 us
    psum x1, blocking collectives, body(): cluster_total, cell_count = lax.psum((part_sums, part_counts), 'recv')  15.8 us
  transfers between devices with their start and end apart: 2, of which 2 were waited for; matrix products, arithmetic and copies ran while one was open for 1% of the time, Pallas kernels for 0%

profile of v1, /device:TPU:1, one launch (start us, length us, event | category | flops | bytes accessed | tf_op | source)
XLA Modules:
  0.0 274.2 jit_solution(15361561997868056688)
XLA Ops:
  6.6 0.0 all-reduce.4.cloned.1.call-start
  6.6 4.6 %fusion.3 = f32[4,128,128]{1,2,0:T(8,128)} fusion(bf16[4,4096,128]{2,1,0:T(8,128)(2,1)} %param.9, s32[4,4096]{1,0:T(4,128)} %param.10), kind=kOutput, calls=%fused_computation.9 | convolution fusion | flops 538968064 | bytes 4521984 | tf_op jit(solution)/shard_map/scg,sck->sgk/dot_general | solution.py:22
  11.2 0.0 all-reduce.4.cloned.1.call-update
  11.2 0.0 all-gather.2.cloned.1.call-start
  11.3 0.0 copy-done.3
  11.3 1.3 convert_reduce_fusion
  12.6 15.8 %psum.45 = f32[4,128]{1,0:T(4,128)S(1)} all-reduce(f32[4,128]{1,0:T(4,128)S(1)} %convert_reduce_fusion), channel_id=1, replica_groups=mesh['samp'=8,'pair'=16,'recv'=4] {'recv'}, use_global_device_ids=true, to_apply=%region_6.7 | all-reduce | flops 512 | bytes 4096 | tf_op jit(solution)/shard_map/psum | solution.py:27
  28.4 48.2 %all-reduce.4.cloned.1.call-done = f32[4,128,128]{1,2,0:T(8,128)} async-done(((f32[4,128,128]{1,2,0:T(8,128)}), f32[4,128,128]{1,2,0:T(8,128)}) %all-reduce.4.cloned.1.call-update) | async-done | bytes 262160 | tf_op jit(solution)/shard_map/psum | solution.py:27
  76.6 1.7 divide_convert_fusion
  78.3 0.0 all-gather.2.cloned.1.call-update
  78.4 0.1 copy.17
  78.5 0.1 fusion.15
  78.7 0.0 copy-done
  78.7 0.2 fusion.16
  78.9 63.7 %all-gather.2.cloned.1.call-done = bf16[4,2048,128]{1,2,0:T(8,128)(2,1)} async-done(((bf16[4,128,128]{1,2,0:T(8,128)(2,1)}), bf16[4,2048,128]{1,2,0:T(8,128)(2,1)}) %all-gather.2.cloned.1.call-update) | async-done | bytes 2097168 | tf_op jit(solution)/shard_map/all_gather | solution.py:29
  142.6 2.0 convolution_convert_fusion
  144.6 1.4 copy.23
  146.0 1.4 convolution_convert_fusion.1
  147.4 2.5 copy.24
  149.9 0.7 gather_fusion
  150.6 2.3 gather_fusion.1
  153.0 0.3 multiply_reduce_fusion
  153.3 64.3 %all-reduce = (f32[4,32]{1,0:T(4,128)S(1)}, f32[32,32]{0,1:T(8,128)S(1)}) all-reduce(f32[4,32]{1,0:T(4,128)S(1)} %multiply_reduce_fusion, f32[32,32]{0,1:T(8,128)S(1)} %fusion.15), channel_id=1, replica_groups=mesh['samp'=8,'pair'=16,'recv'=4] {'pair'}, use_global_device_ids=true, to_apply=%region_8.10 | all-reduce | flops 1152 | bytes 9216 | tf_op jit(solution)/shard_map/psum | solution.py:55
  217.6 41.8 %all-reduce.1 = (f32[4,32]{1,0:T(4,128)S(1)}, f32[32,32]{0,1:T(8,128)S(1)}) all-reduce(f32[4,32]{1,0:T(4,128)S(1)} %get-tuple-element.6, f32[32,32]{0,1:T(8,128)S(1)} %fusion.16), channel_id=1, replica_groups=mesh['samp'=8,'pair'=16,'recv'=4] {'recv'}, use_global_device_ids=true, to_apply=%region_9.11 | all-reduce | flops 1152 | bytes 9216 | tf_op jit(solution)/shard_map/psum | solution.py:55
  259.4 0.1 fusion.4
  259.5 0.1 copy.16
  259.6 2.9 %cholesky.16 = f32[32,32]{1,0:T(8,128)S(1)} custom-call(f32[32,32]{1,0:T(8,128)S(1)} %fusion.11), custom_call_target="Cholesky" | custom-call | tf_op jit(solution)/shard_map/jit(cholesky)/cholesky | solution.py:59
  262.6 0.6 compare_reduce_fusion
  263.2 0.7 fusion.6
  263.9 2.4 custom-call.10
  266.3 0.2 fusion.9
  266.6 0.8 fusion.7
  (19 shorter events, 0.1 us)
Async XLA Ops:
  6.5 72.1 %copy-start = (bf16[32,32]{1,0:T(8,128)(2,1)S(1)}, bf16[32,32]{1,0:T(8,128)(2,1)}, u32[]{:S(2)}) copy-start(bf16[32,32]{1,0:T(8,128)(2,1)} %param.15) | copy-start | bytes 6148
  6.5 4.8 %copy-start.3 = (s32[4,4096]{1,0:T(4,128)S(1)}, s32[4,4096]{1,0:T(4,128)}, u32[]{:S(2)}) copy-start(s32[4,4096]{1,0:T(4,128)} %param.10) | copy-start | bytes 196612
  6.5 71.8 %copy-start.2 = (bf16[128,32]{0,1:T(8,128)(2,1)S(1)}, bf16[128,32]{0,1:T(8,128)(2,1)}, u32[]{:S(2)}) copy-start(bf16[128,32]{0,1:T(8,128)(2,1)} %param.13) | copy-start | bytes 24580
  6.5 71.9 %copy-start.4 = (s32[128]{0:T(128)S(1)}, s32[128]{0:T(128)}, u32[]{:S(2)}) copy-start(s32[128]{0:T(128)} %param.12) | copy-start | bytes 1540
  6.5 71.9 %copy-start.5 = (s32[128]{0:T(128)S(1)}, s32[128]{0:T(128)}, u32[]{:S(2)}) copy-start(s32[128]{0:T(128)} %param.11) | copy-start | bytes 1540
  6.5 136.0 %copy-start.1 = (bf16[128,32]{0,1:T(8,128)(2,1)S(1)}, bf16[128,32]{0,1:T(8,128)(2,1)}, u32[]{:S(2)}) copy-start(bf16[128,32]{0,1:T(8,128)(2,1)} %param.14) | copy-start | bytes 24580
  6.6 70.0 %all-reduce.4.cloned.1.call-start = ((), (), s32[]{:S(2)}) async-start(), calls=%async_computation | async-start | bytes 524288 | tf_op jit(solution)/shard_map/psum | solution.py:27
  11.2 131.3 %all-gather.2.cloned.1.call-start = ((), (), s32[]{:S(2)}) async-start(), calls=%async_computation.1 | async-start | bytes 2228224 | tf_op jit(solution)/shard_map/all_gather | solution.py:29
Sparse Core Ops, SparseCore 0:
  11.4 65.1 all-reduce.3
  78.8 63.7 all-gather.1
